TPU v7x, 256 devices: a whole 4x4x8 slice. The times are simulated.
256 devices in a mesh: occ: 16 (over z, y_hi), aux: 16 (over y_lo, x, core).
Axes of the slice: x: 4, y: 4 (y_hi: 2, y_lo: 2; y = y_hi * 2 + y_lo), z: 8, core: 2. Of those that a mesh axis runs over, the one named last changes fastest.
Arguments:
- orbital_b: bfloat16 [128, 3072, 768], P('occ', 'aux'), may hold values from -0.75 to 0.75
- occ_energy: float32 [128], replicated, may hold values from -3 to -0.5
- vir_energy: float32 [768], replicated, may hold values from 0.2 to 3
Outputs:
- gradient_term: bfloat16 [128, 3072, 768], P('occ', 'aux')
All inputs are finite; a program needn't handle non-finite values.
Results may differ from a plain program's by a relative error of at most 0.0044.
Values may be sent and summed in bfloat16 or wider, within the bound.
A program may use at most 64 MiB of HBM per device.

v0:
```python
import jax
import jax.numpy as jnp
from jax import lax
from jax.sharding import PartitionSpec as P


def shifted(value, axis, steps):
    count = lax.axis_size(axis)
    initial, last = (max(0, -steps), min(count, count - steps))
    return lax.ppermute(value, axis, [(source, source + steps) for source in range(initial, last)])


def shards(orbital_b, occ_energy, vir_energy):
    occ_index = lax.axis_index("occ")
    aux_index = lax.axis_index("aux")
    occ_count = lax.axis_size("occ")
    block_rows = orbital_b.shape[0]
    vir_width = orbital_b.shape[2]
    slab_width = vir_width // lax.axis_size("aux")
    columns = lax.all_to_all(orbital_b, "aux", split_axis=2, concat_axis=1, tiled=True)
    own_energy = lax.dynamic_slice_in_dim(occ_energy, occ_index * block_rows, block_rows)
    vir_slab = lax.dynamic_slice_in_dim(vir_energy, aux_index * slab_width, slab_width)
    energy_left = occ_energy[jnp.maximum(occ_index - 1, 0) * block_rows]
    energy_right = occ_energy[jnp.minimum(occ_index + 1, occ_count - 1) * block_rows]
    partner_energy = jnp.stack([energy_left, energy_right])
    leading = columns[:1]
    from_left_block = shifted(leading, "occ", 1)
    from_right_block = shifted(leading, "occ", -1)
    partners = jnp.concatenate([from_left_block, from_right_block], axis=0)
    segment = lax.all_gather(partners, "aux", axis=2, tiled=True)
    integral = jnp.einsum("iPa,pPb->iapb", columns, segment, preferred_element_type=jnp.float32)
    denominator = (
        vir_slab[None, :, None, None]
        + vir_energy[None, None, None, :]
        - own_energy[:, None, None, None]
        - partner_energy[None, None, :, None]
    )
    amplitude = (integral / denominator).astype(jnp.bfloat16)
    running = jnp.einsum("iapb,pPb->iPa", amplitude, segment, preferred_element_type=jnp.float32)
    gradient_slab = running.astype(jnp.bfloat16)
    return lax.all_to_all(gradient_slab, "aux", split_axis=1, concat_axis=2, tiled=True)


def solution(mesh):
    placed = (P("occ", "aux", None), P(), P())
    return jax.shard_map(
        shards, mesh=mesh, in_specs=placed, out_specs=P("occ", "aux", None), check_vma=False
    )
```

profile of v0, /device:TPU:1, one launch (start us, length us, event | category | flops | bytes accessed | tf_op | source)
XLA Modules:
  0.0 229.1 jit_solution(18051163929910925184)
XLA Ops:
  6.5 0.0 all-gather.2.cloned.1.call-start
  6.5 5.0 %copy.15 = bf16[8,192,768]{1,0,2:T(8,128)(2,1)} copy(bf16[8,192,768]{2,1,0:T(8,128)(2,1)} %param.3) | data formatting | bytes 4718592 | tf_op args[0]
  11.6 44.4 %all_to_all.36 = bf16[8,192,768]{1,0,2:T(8,128)(2,1)S(1)} all-to-all(bf16[8,192,768]{1,0,2:T(8,128)(2,1)} %copy.15), channel_id=1, replica_groups=mesh['occ'=16,'aux'=16] {'aux'}, dimensions={2} | all-to-all | bytes 4718592 | tf_op jit(solution)/shard_map/all_to_all | solution.py:20
  55.9 0.6 copy.16
  56.6 0.0 copy-start.1
  56.6 0.0 copy-start
  56.7 0.1 copy.17
  56.8 1.1 slice.7
  57.9 1.3 collective-permute-start.1
  59.2 5.5 %collective-permute-start = (bf16[1,3072,48]{1,2,0:T(8,128)(2,1)}, bf16[1,3072,48]{1,2,0:T(8,128)(2,1)S(1)}, u32[]{:S(2)}, u32[]{:S(2)}) collective-permute-start(bf16[1,3072,48]{1,2,0:T(8,128)(2,1)} %slice.7), channel_id=1, source_target_pairs={{0,16},{16,32},{32,48},{48,64},{64,80},{80,96},{96,112},{112,128},... | collective-permute-start | bytes 884744 | tf_op jit(solution)/shard_map/ppermute | solution.py:10
  64.7 3.9 %collective-permute-done.1 = bf16[1,3072,48]{1,2,0:T(8,128)(2,1)S(1)} collective-permute-done((bf16[1,3072,48]{1,2,0:T(8,128)(2,1)}, bf16[1,3072,48]{1,2,0:T(8,128)(2,1)S(1)}, u32[]{:S(2)}, u32[]{:S(2)}) %collective-permute-start.1) | collective-permute-done | bytes 294944 | tf_op jit(solution)/shard_map/ppermute | solution.py:10
  68.6 8.0 %collective-permute-done = bf16[1,3072,48]{1,2,0:T(8,128)(2,1)S(1)} collective-permute-done((bf16[1,3072,48]{1,2,0:T(8,128)(2,1)}, bf16[1,3072,48]{1,2,0:T(8,128)(2,1)S(1)}, u32[]{:S(2)}, u32[]{:S(2)}) %collective-permute-start) | collective-permute-done | bytes 294944 | tf_op jit(solution)/shard_map/ppermute | solution.py:10
  76.6 0.9 pad_maximum_fusion
  77.5 0.0 all-gather.2.cloned.1.call-update
  77.6 0.0 copy-done.1
  77.6 0.1 dynamic_slice.13
  77.7 0.0 copy-done
  77.7 0.1 dynamic_slice.12
  77.7 0.6 fusion.15
  78.4 1.3 pad_maximum_fusion.1
  79.7 0.1 broadcast_add_fusion
  79.8 1.2 broadcast_subtract_fusion
  81.0 3.4 %copy.18 = bf16[8,16,192,48]{2,1,3,0:T(8,128)(2,1)} copy(bf16[8,16,192,48]{2,0,3,1:T(8,128)(2,1)S(1)} %bitcast.46) | data formatting | bytes 4718592 | tf_op jit(solution)/shard_map/all_to_all | solution.py:20
  84.4 5.1 %reshape.41 = bf16[8,3072,48,1]{1,2,0,3:T(8,128)(2,1)S(1)} reshape(bf16[8,16,192,48]{2,1,3,0:T(8,128)(2,1)} %copy.18) | data formatting | bytes 4718592 | tf_op jit(solution)/shard_map/all_to_all | solution.py:20
  89.5 50.5 %all-gather.2.cloned.1.call-done = bf16[2,3072,768]{1,2,0:T(8,128)(2,1)} async-done(((bf16[2,3072,48]{1,2,0:T(8,128)(2,1)}), bf16[2,3072,768]{1,2,0:T(8,128)(2,1)}) %all-gather.2.cloned.1.call-update) | async-done | bytes 9437200 | tf_op jit(solution)/shard_map/all_gather | solution.py:30
  140.0 0.0 copy-start.2
  140.0 8.0 %fusion.9 = bf16[8,48,2,768]{3,1,2,0:T(8,128)(2,1)S(1)} fusion(bf16[8,3072,48,1]{1,2,0,3:T(8,128)(2,1)S(1)} %reshape.41, bf16[2,3072,768]{1,2,0:T(8,128)(2,1)} %all-gather.2.cloned.1.call-done, f32[2]{0:T(128)S(1)} %pad_maximum_fusion.1, f32[8,48,768]{2,1,0:T(8,128)} %broadcast_subtract_fusion), kind=kOutput, calls=%fused_computation.7 | convolution fusion | flops 3625648128 | bytes 14155784 | tf_op jit(solution)/shard_map/iPa,pPb->iapb/dot_general | solution.py:31
  147.9 0.0 copy-done.2
  148.0 4.2 %fusion.6 = bf16[8,3072,48]{1,2,0:T(8,128)(2,1)S(1)} fusion(bf16[8,48,2,768]{3,1,2,0:T(8,128)(2,1)S(1)} %fusion.9, bf16[2,3072,768]{1,2,0:T(8,128)(2,1)S(1)} %copy-done.2), kind=kOutput, calls=%fused_computation.5 | convolution fusion | flops 3625058304 | bytes 12976128 | tf_op jit(solution)/shard_map/iapb,pPb->iPa/dot_general | solution.py:39
  152.1 6.0 %copy.19 = bf16[8,3072,48]{2,0,1:T(8,128)(2,1)} copy(bf16[8,3072,48]{1,2,0:T(8,128)(2,1)S(1)} %fusion.6) | data formatting | bytes 4718592 | tf_op jit(solution)/shard_map/convert_element_type | solution.py:40
  158.1 10.3 %reshape.44 = bf16[16,2,36864]{2,1,0:T(2,128)(2,1)S(1)} reshape(bf16[3072,8,48]{2,1,0:T(8,128)(2,1)} %bitcast.48) | data formatting | bytes 4718592
  168.4 34.7 %all_to_all.37 = bf16[16,2,36864]{2,1,0:T(2,128)(2,1)} all-to-all(bf16[16,2,36864]{2,1,0:T(2,128)(2,1)S(1)} %reshape.44), channel_id=1, replica_groups=mesh['occ'=16,'aux'=16] {'aux'}, dimensions={0} | all-to-all | bytes 4718592 | tf_op jit(solution)/shard_map/all_to_all | solution.py:41
  203.2 9.2 %reshape.45 = bf16[3072,8,48]{2,1,0:T(8,128)(2,1)} reshape(bf16[16,2,36864]{2,1,0:T(2,128)(2,1)} %all_to_all.37) | data formatting | bytes 4718592
  212.4 7.2 %copy.20 = bf16[8,16,192,48]{2,3,1,0:T(8,128)(2,1)S(1)} copy(bf16[8,16,192,48]{3,0,2,1:T(8,128)(2,1)} %bitcast.47) | data formatting | bytes 4718592 | tf_op jit(solution)/shard_map/all_to_all | solution.py:41
  219.6 2.6 %copy.21 = bf16[8,192,768]{2,1,0:T(8,128)(2,1)} copy(bf16[8,192,768]{1,2,0:T(8,128)(2,1)S(1)} %bitcast.49) | data formatting | bytes 4718592 | tf_op jit(solution)/shard_map/all_to_all | solution.py:41
  (1 shorter events, 0.0 us)
Async XLA Ops:
  6.5 133.4 %all-gather.2.cloned.1.call-start = ((), (), s32[]{:S(2)}) async-start(), calls=%async_computation.2 | async-start | bytes 10027008 | tf_op jit(solution)/shard_map/all_gather | solution.py:30
  56.6 21.0 %copy-start.1 = (f32[128]{0:T(128)S(1)}, f32[128]{0:T(128)}, u32[]{:S(2)}) copy-start(f32[128]{0:T(128)} %param.4) | copy-start | bytes 1540
  56.6 21.0 %copy-start = (f32[768]{0:T(1024)S(1)}, f32[768]{0:T(1024)}, u32[]{:S(2)}) copy-start(f32[768]{0:T(1024)} %param.5) | copy-start | bytes 9220
  57.9 10.7 %collective-permute-start.1 = (bf16[1,3072,48]{1,2,0:T(8,128)(2,1)}, bf16[1,3072,48]{1,2,0:T(8,128)(2,1)S(1)}, u32[]{:S(2)}, u32[]{:S(2)}) collective-permute-start(bf16[1,3072,48]{1,2,0:T(8,128)(2,1)} %slice.7), channel_id=1, source_target_pairs={{16,0},{32,16},{48,32},{64,48},{80,64},{96,80},{112,96},{128,112},... | collective-permute-start | bytes 884744 | tf_op jit(solution)/shard_map/ppermute | solution.py:10
  59.2 17.5 %collective-permute-start = (bf16[1,3072,48]{1,2,0:T(8,128)(2,1)}, bf16[1,3072,48]{1,2,0:T(8,128)(2,1)S(1)}, u32[]{:S(2)}, u32[]{:S(2)}) collective-permute-start(bf16[1,3072,48]{1,2,0:T(8,128)(2,1)} %slice.7), channel_id=1, source_target_pairs={{0,16},{16,32},{32,48},{48,64},{64,80},{80,96},{96,112},{112,128},... | collective-permute-start | bytes 884744 | tf_op jit(solution)/shard_map/ppermute | solution.py:10
  140.0 8.0 %copy-start.2 = (bf16[2,3072,768]{1,2,0:T(8,128)(2,1)S(1)}, bf16[2,3072,768]{1,2,0:T(8,128)(2,1)}, u32[]{:S(2)}) copy-start(bf16[2,3072,768]{1,2,0:T(8,128)(2,1)} %all-gather.2.cloned.1.call-done) | copy-start | bytes 28311556
Sparse Core Ops, SparseCore 0:
  77.7 62.2 all-gather.1
where the time goes:
time: 230 us; the launch traced here: 229 us
  blocking collectives  79.1 us (34%)
  waiting for transfers between devices  62.5 us (27%)
  local copies, waits for them, and re-layouts  51.5 us (22%)
  between operations  13.5 us (6%)
  matrix products  12.1 us (5%)
  starting transfers between devices  6.79 us (3%)
  other arithmetic  3.49 us (2%)
    all_gather x1, waiting for transfers between devices, shards(): segment = lax.all_gather(partners, 'aux', axis=2, tiled=True)  50.5 us
    all_to_all x1, blocking collectives, shards(): lax.all_to_all(orbital_b, 'aux', split_axis=2, concat_axis=1, tiled=True)  44.4 us
    all_to_all x1, blocking collectives, shards(): lax.all_to_all(gradient_slab, 'aux', split_axis=1, concat_axis=2, tiled=T...  34.7 us
    unnamed x9, local copies, waits for them, and re-layouts  24.6 us
    ppermute x2, waiting for transfers between devices, shifted(): lax.ppermute(value, axis, [(source, source + steps) for source in range(i...  12 us
    all_to_all x2, local copies, waits for them, and re-layouts, shards(): lax.all_to_all(gradient_slab, 'aux', split_axis=1, concat_axis=2, tiled=T...  9.8 us
    all_to_all x3, local copies, waits for them, and re-layouts, shards(): lax.all_to_all(orbital_b, 'aux', split_axis=2, concat_axis=1, tiled=True)  9.12 us
    dot_general x1, matrix products, shards(): jnp.einsum('iPa,pPb->iapb', columns, segment, preferred_element_type=jnp....  7.96 us
  transfers between devices with their start and end apart: 3, of which 3 were waited for; matrix products, arithmetic and copies ran while one was open for 5% of the time, Pallas kernels for 0%

commit v1 on v0

--- a/solution.py
+++ b/solution.py
@@ -27,7 +27,9 @@
     from_left_block = shifted(leading, "occ", 1)
     from_right_block = shifted(leading, "occ", -1)
     partners = jnp.concatenate([from_left_block, from_right_block], axis=0)
-    segment = lax.all_gather(partners, "aux", axis=2, tiled=True)
+    segment = jnp.concatenate(
+        lax.all_to_all(jnp.stack([partners] * lax.axis_size("aux")), "aux", 0, 0), axis=2
+    )
     integral = jnp.einsum("iPa,pPb->iapb", columns, segment, preferred_element_type=jnp.float32)
     denominator = (
         vir_slab[None, :, None, None]

time: 230 us -> 300 us (1.30)
  waiting for transfers between devices: 62.5 us -> 126 us
  local copies, waits for them, and re-layouts: 51.5 us -> 65.1 us
  between operations: 13.5 us -> 0.11 us
  starting transfers between devices: 6.79 us -> 11.9 us
    all_to_all x0 -> x1, waiting for transfers between devices: none -> 114 us  [shards(): lax.all_to_all(jnp.stack([partners] * lax.axis_size('aux')), 'aux', 0, 0)]
    all_gather x1 -> x0, waiting for transfers between devices: 50.5 us -> none  [shards(): segment = lax.all_gather(partners, 'aux', axis=2, tiled=True)]
    all_to_all x0 -> x1, local copies, waits for them, and re-layouts: none -> 8.71 us  [shards(): lax.all_to_all(jnp.stack([partners] * lax.axis_size('aux')), 'aux', 0, 0)]
    all_to_all x0 -> x1, starting transfers between devices: none -> 5.14 us  [shards(): lax.all_to_all(jnp.stack([partners] * lax.axis_size('aux')), 'aux', 0, 0)]
    another operation x0 -> x1, local copies, waits for them, and re-layouts: none -> 4.84 us  [shards(): jnp.stack([partners] * lax.axis_size('aux'))]
  transfers between devices with their start and end apart: 3 -> 3, of which waited for: 3 -> 3; matrix products, arithmetic and copies ran while one was open for 5% -> 4% of each run, Pallas kernels for 0% -> 0%
where the time goes in v1:
time: 300 us; the launch traced here: 297 us
  waiting for transfers between devices  126 us (42%)
  blocking collectives  79.4 us (26%)
  local copies, waits for them, and re-layouts  65.1 us (22%)
  matrix products  12.1 us (4%)
  starting transfers between devices  11.9 us (4%)
    all_to_all x1, waiting for transfers between devices, shards(): lax.all_to_all(jnp.stack([partners] * lax.axis_size('aux')), 'aux', 0, 0)  114 us
    all_to_all x1, blocking collectives, shards(): lax.all_to_all(orbital_b, 'aux', split_axis=2, concat_axis=1, tiled=True)  44.4 us
    all_to_all x1, blocking collectives, shards(): lax.all_to_all(gradient_slab, 'aux', split_axis=1, concat_axis=2, tiled=T...  35 us
    unnamed x9, local copies, waits for them, and re-layouts  24.6 us
    ppermute x2, waiting for transfers between devices, shifted(): lax.ppermute(value, axis, [(source, source + steps) for source in range(i...  12 us
    all_to_all x2, local copies, waits for them, and re-layouts, shards(): lax.all_to_all(gradient_slab, 'aux', split_axis=1, concat_axis=2, tiled=T...  9.8 us
    all_to_all x3, local copies, waits for them, and re-layouts, shards(): lax.all_to_all(orbital_b, 'aux', split_axis=2, concat_axis=1, tiled=True)  9.14 us
    all_to_all x1, local copies, waits for them, and re-layouts, shards(): lax.all_to_all(jnp.stack([partners] * lax.axis_size('aux')), 'aux', 0, 0)  8.71 us
  transfers between devices with their start and end apart: 3, of which 3 were waited for; matrix products, arithmetic and copies ran while one was open for 4% of the time, Pallas kernels for 0%

profile of v1, /device:TPU:1, one launch (start us, length us, event | category | flops | bytes accessed | tf_op | source)
XLA Modules:
  0.0 297.5 jit_solution(13894136112145120838)
XLA Ops:
  0.0 5.0 %copy.11 = bf16[8,192,768]{1,0,2:T(8,128)(2,1)} copy(bf16[8,192,768]{2,1,0:T(8,128)(2,1)} %param.3) | data formatting | bytes 4718592 | tf_op args[0]
  5.0 44.4 %all_to_all.41 = bf16[8,192,768]{1,0,2:T(8,128)(2,1)S(1)} all-to-all(bf16[8,192,768]{1,0,2:T(8,128)(2,1)} %copy.11), channel_id=1, replica_groups=mesh['occ'=16,'aux'=16] {'aux'}, dimensions={2} | all-to-all | bytes 4718592 | tf_op jit(solution)/shard_map/all_to_all | solution.py:20
  49.4 0.6 copy.12
  50.1 0.1 copy.13
  50.2 1.1 slice.7
  51.3 1.3 collective-permute-start.1
  52.6 5.5 %collective-permute-start = (bf16[1,3072,48]{1,2,0:T(8,128)(2,1)}, bf16[1,3072,48]{1,2,0:T(8,128)(2,1)S(1)}, u32[]{:S(2)}, u32[]{:S(2)}) collective-permute-start(bf16[1,3072,48]{1,2,0:T(8,128)(2,1)} %slice.7), channel_id=1, source_target_pairs={{0,16},{16,32},{32,48},{48,64},{64,80},{80,96},{96,112},{112,128},... | collective-permute-start | bytes 884744 | tf_op jit(solution)/shard_map/ppermute | solution.py:10
  58.1 3.9 %collective-permute-done.1 = bf16[1,3072,48]{1,2,0:T(8,128)(2,1)S(1)} collective-permute-done((bf16[1,3072,48]{1,2,0:T(8,128)(2,1)}, bf16[1,3072,48]{1,2,0:T(8,128)(2,1)S(1)}, u32[]{:S(2)}, u32[]{:S(2)}) %collective-permute-start.1) | collective-permute-done | bytes 294944 | tf_op jit(solution)/shard_map/ppermute | solution.py:10
  62.0 8.0 %collective-permute-done = bf16[1,3072,48]{1,2,0:T(8,128)(2,1)S(1)} collective-permute-done((bf16[1,3072,48]{1,2,0:T(8,128)(2,1)}, bf16[1,3072,48]{1,2,0:T(8,128)(2,1)S(1)}, u32[]{:S(2)}, u32[]{:S(2)}) %collective-permute-start) | collective-permute-done | bytes 294944 | tf_op jit(solution)/shard_map/ppermute | solution.py:10
  70.1 0.1 pad_maximum_fusion
  70.1 4.8 %stack.4 = bf16[16,2,3072,48]{2,3,1,0:T(8,128)(2,1)} broadcast(bf16[2,3072,48]{1,2,0:T(8,128)(2,1)S(1)} %pad_maximum_fusion), dimensions={1,2,3} | broadcast | bytes 10027008 | tf_op jit(solution)/shard_map/stack | solution.py:31
  75.0 0.0 copy-start.2
  75.0 0.0 copy-start.1
  75.0 5.1 %all-to-all-start.1 = ((bf16[16,2,3072,48]{2,3,1,0:T(8,128)(2,1)}), bf16[16,2,3072,48]{2,3,1,0:T(8,128)(2,1)}, u32[]{:S(2)}, u32[]{:S(2)}) async-start(bf16[16,2,3072,48]{2,3,1,0:T(8,128)(2,1)} %stack.4), calls=%async_computation.1 | async-start | bytes 18874368 | tf_op jit(solution)/shard_map/all_to_all | solution.py:31
  80.1 0.0 copy-done.2
  80.1 0.1 dynamic_slice.13
  80.2 0.0 copy-done.1
  80.2 0.1 dynamic_slice.12
  80.3 0.7 fusion.6
  80.9 1.4 pad_maximum_fusion.1
  82.3 0.1 broadcast_add_fusion
  82.4 1.2 broadcast_subtract_fusion
  83.6 3.4 %copy.15 = bf16[8,16,192,48]{2,1,3,0:T(8,128)(2,1)} copy(bf16[8,16,192,48]{2,0,3,1:T(8,128)(2,1)S(1)} %bitcast.43) | data formatting | bytes 4718592 | tf_op jit(solution)/shard_map/all_to_all | solution.py:20
  87.0 5.1 %reshape.51 = bf16[8,3072,48,1]{1,2,0,3:T(8,128)(2,1)S(1)} reshape(bf16[8,16,192,48]{2,1,3,0:T(8,128)(2,1)} %copy.15) | data formatting | bytes 4718592 | tf_op jit(solution)/shard_map/all_to_all | solution.py:20
  92.1 114.1 %all-to-all-done.1 = bf16[16,2,3072,48]{2,3,1,0:T(8,128)(2,1)} async-done(((bf16[16,2,3072,48]{2,3,1,0:T(8,128)(2,1)}), bf16[16,2,3072,48]{2,3,1,0:T(8,128)(2,1)}, u32[]{:S(2)}, u32[]{:S(2)}) %all-to-all-start.1) | async-done | bytes 9437216 | tf_op jit(solution)/shard_map/all_to_all | solution.py:31
  206.2 8.7 %copy.14 = bf16[16,2,3072,48]{2,3,0,1:T(8,128)(2,1)} copy(bf16[16,2,3072,48]{2,3,1,0:T(8,128)(2,1)} %all-to-all-done.1) | data formatting | bytes 18874368 | tf_op jit(solution)/shard_map/all_to_all | solution.py:31
  214.9 0.0 copy-start
  214.9 8.0 %fusion.1 = bf16[8,48,2,768]{3,1,2,0:T(8,128)(2,1)S(1)} fusion(bf16[2,3072,768,1]{1,2,0,3:T(8,128)(2,1)} %bitcast.47, bf16[8,3072,48,1]{1,2,0,3:T(8,128)(2,1)S(1)} %reshape.51, f32[2]{0:T(128)S(1)} %pad_maximum_fusion.1, f32[8,48,768]{2,1,0:T(8,128)} %broadcast_subtract_fusion), kind=kOutput, calls=%fused_computation.3 | convolution fusion | flops 3625648128 | bytes 14155784 | tf_op jit(solution)/shard_map/iPa,pPb->iapb/dot_general | solution.py:33
  222.9 0.0 copy-done
  222.9 4.2 %fusion = bf16[8,3072,48]{1,2,0:T(8,128)(2,1)S(1)} fusion(bf16[2,3072,768,1]{1,2,0,3:T(8,128)(2,1)S(1)} %bitcast.48, bf16[8,48,2,768]{3,1,2,0:T(8,128)(2,1)S(1)} %fusion.1), kind=kOutput, calls=%fused_computation.1 | convolution fusion | flops 3625058304 | bytes 12976128 | tf_op jit(solution)/shard_map/iapb,pPb->iPa/dot_general | solution.py:41
  227.1 6.0 %copy.18 = bf16[8,3072,48]{2,0,1:T(8,128)(2,1)} copy(bf16[8,3072,48]{1,2,0:T(8,128)(2,1)S(1)} %fusion) | data formatting | bytes 4718592 | tf_op jit(solution)/shard_map/convert_element_type | solution.py:42
  233.1 10.3 %reshape.55 = bf16[16,2,36864]{2,1,0:T(2,128)(2,1)S(1)} reshape(bf16[3072,8,48]{2,1,0:T(8,128)(2,1)} %bitcast.45) | data formatting | bytes 4718592
  243.4 35.0 %all_to_all.42 = bf16[16,2,36864]{2,1,0:T(2,128)(2,1)} all-to-all(bf16[16,2,36864]{2,1,0:T(2,128)(2,1)S(1)} %reshape.55), channel_id=1, replica_groups=mesh['occ'=16,'aux'=16] {'aux'}, dimensions={0} | all-to-all | bytes 4718592 | tf_op jit(solution)/shard_map/all_to_all | solution.py:43
  278.4 9.2 %reshape.56 = bf16[3072,8,48]{2,1,0:T(8,128)(2,1)} reshape(bf16[16,2,36864]{2,1,0:T(2,128)(2,1)} %all_to_all.42) | data formatting | bytes 4718592
  287.7 7.2 %copy.19 = bf16[8,16,192,48]{2,3,1,0:T(8,128)(2,1)S(1)} copy(bf16[8,16,192,48]{3,0,2,1:T(8,128)(2,1)} %bitcast.44) | data formatting | bytes 4718592 | tf_op jit(solution)/shard_map/all_to_all | solution.py:43
  294.9 2.6 copy.20
  (1 shorter events, 0.0 us)
Async XLA Ops:
  51.3 10.7 %collective-permute-start.1 = (bf16[1,3072,48]{1,2,0:T(8,128)(2,1)}, bf16[1,3072,48]{1,2,0:T(8,128)(2,1)S(1)}, u32[]{:S(2)}, u32[]{:S(2)}) collective-permute-start(bf16[1,3072,48]{1,2,0:T(8,128)(2,1)} %slice.7), channel_id=1, source_target_pairs={{16,0},{32,16},{48,32},{64,48},{80,64},{96,80},{112,96},{128,112},... | collective-permute-start | bytes 884744 | tf_op jit(solution)/shard_map/ppermute | solution.py:10
  52.6 17.5 %collective-permute-start = (bf16[1,3072,48]{1,2,0:T(8,128)(2,1)}, bf16[1,3072,48]{1,2,0:T(8,128)(2,1)S(1)}, u32[]{:S(2)}, u32[]{:S(2)}) collective-permute-start(bf16[1,3072,48]{1,2,0:T(8,128)(2,1)} %slice.7), channel_id=1, source_target_pairs={{0,16},{16,32},{32,48},{48,64},{64,80},{80,96},{96,112},{112,128},... | collective-permute-start | bytes 884744 | tf_op jit(solution)/shard_map/ppermute | solution.py:10
  75.0 5.1 %copy-start.2 = (f32[128]{0:T(128)S(1)}, f32[128]{0:T(128)}, u32[]{:S(2)}) copy-start(f32[128]{0:T(128)} %param.4) | copy-start | bytes 1540
  75.0 5.2 %copy-start.1 = (f32[768]{0:T(1024)S(1)}, f32[768]{0:T(1024)}, u32[]{:S(2)}) copy-start(f32[768]{0:T(1024)} %param.5) | copy-start | bytes 9220
  75.0 131.2 %all-to-all-start.1 = ((bf16[16,2,3072,48]{2,3,1,0:T(8,128)(2,1)}), bf16[16,2,3072,48]{2,3,1,0:T(8,128)(2,1)}, u32[]{:S(2)}, u32[]{:S(2)}) async-start(bf16[16,2,3072,48]{2,3,1,0:T(8,128)(2,1)} %stack.4), calls=%async_computation.1 | async-start | bytes 18874368 | tf_op jit(solution)/shard_map/all_to_all | solution.py:31
  214.9 8.0 %copy-start = (bf16[16,2,3072,48]{2,3,0,1:T(8,128)(2,1)S(1)}, bf16[16,2,3072,48]{2,3,0,1:T(8,128)(2,1)}, u32[]{:S(2)}) copy-start(bf16[16,2,3072,48]{2,3,0,1:T(8,128)(2,1)} %copy.14) | copy-start | bytes 28311556
